TPU v7x, 32 devices: a whole 2x2x4 slice. The times are simulated.
32 devices in a mesh: gx: 2 (over core), gy: 4 (over z), gz: 4 (over y, x).
Axes of the slice: x: 2, y: 2, z: 4, core: 2. Of those that a mesh axis runs over, the one named last changes fastest.
Arguments:
- positions: float32 [2, 4, 4, 2, 3, 128], P('gx', 'gy', 'gz'), may hold values from 0 to 12, as said below
- features: bfloat16 [2, 4, 4, 2, 128, 128], P('gx', 'gy', 'gz'), may hold values from -6 to 6
- counts: int32 [2, 4, 4, 2], P('gx', 'gy', 'gz'), may hold values from 0 to 128, as said below
- neighbours: int32 [2, 4, 4, 2, 8], P('gx', 'gy', 'gz'), may hold values from -1 to 53, as said below
- mix_weight: bfloat16 [1024, 128], replicated, may hold values from -0.1875 to 0.1875
- readout: float32 [128], replicated, may hold values from -4 to 4
- radial_rates: float32 [4], replicated, may hold values from 0.03 to 0.6
Outputs:
- forces: float32 [2, 4, 4, 2, 3, 128], P('gx', 'gy', 'gz')
- feature_grads: float32 [2, 4, 4, 2, 128, 128], P('gx', 'gy', 'gz')
Inputs may be any that keep to these rules, and one draw needn't show every extreme that they name: The atoms of a tile fill its first counts slots; a count of 0 marks a tile slot that its device doesn't own; every draw has a tile with 128 atoms. neighbours[.., t, s] names a tile of the device's neighbourhood as ((dx + 1) * 9 + (dy + 1) * 3 + (dz + 1)) * 2 + u, dx, dy, dz in -1..1 being the device offsets along gx, gy, gz and u the tile slot; slot 0 names tile t itself, every other used slot names a tile with one or more atoms, the entries of a row differ, and -1 marks unused slots, which come after the used ones. `positions`: the atoms of device (a, b, c) lie in the cube of side 3 whose lowest corner is 3 (a, b, c).
All inputs are finite; a program needn't handle non-finite values.
Results may differ from a plain program's by a relative error of at most 0.0008.
Values may be sent and summed in bfloat16 or wider, within the bound.
No kernel may reach another device: no remote copies, remote signals or barrier semaphores. Data moves between devices by JAX's collectives and lax.ppermute only.
A program may use at most 64 MiB of HBM per device.

v0:
```python
import jax
import jax.numpy as jnp
from jax import lax
from jax.sharding import PartitionSpec as P


def extended(block, sides, width):
    for axis, dim in sides:
        count = lax.axis_size(axis)
        forward = [(i, i + 1) for i in range(count - 1)]
        backward = [(target, source) for source, target in forward]
        low = lax.ppermute(
            lax.slice_in_dim(block, block.shape[dim] - width, None, axis=dim), axis, forward
        )
        high = lax.ppermute(lax.slice_in_dim(block, 0, width, axis=dim), axis, backward)
        block = jnp.concatenate([low, block, high], axis=dim)
    return block


def from_behind(block, axis, distance):
    devices = range(lax.axis_size(axis))
    route = [(i - distance, i) for i in devices if i - distance in devices]
    return lax.ppermute(block, axis, route)


def build_basis(own_points, other_points, decay_rates):
    offset = other_points[None, :, :] - jnp.transpose(own_points)[:, :, None]
    square_dist = jnp.sum(offset * offset, axis=1)
    radial = jnp.exp(-decay_rates[None, :, None] * square_dist[:, None, :])
    pair_basis = jnp.concatenate(
        [radial[:, :, None, :], radial[:, :, None, :] * offset[:, None, :, :]], axis=2
    )
    return (offset, radial, pair_basis)


def device_terms(
    own_points,
    own_valid,
    own_counts,
    near_points,
    near_features,
    neighbour_rows,
    mixing,
    readout,
    decay_rates,
):
    tile_count = own_points.shape[0]
    atom_count = own_points.shape[2]
    channel_count = near_features.shape[2]
    slot_count = neighbour_rows.shape[1]
    radial_count = decay_rates.shape[0]
    basis_count = 4 * radial_count
    scaling = (slot_count * atom_count) ** (-0.5)
    pair_count = tile_count * slot_count
    row_width = (3 + channel_count) * atom_count

    def locate(pair_index):
        tile_index = pair_index // slot_count
        slot_index = pair_index % slot_count
        target = neighbour_rows[tile_index, slot_index]
        is_live = target >= 0
        source_index = jnp.maximum(target, 0)
        active = is_live & (own_counts[tile_index] > 0)
        return (tile_index, source_index, is_live, active)

    def forward_pair(pair_index, summed):
        tile_index, source_index, is_live, active = locate(pair_index)
        near_tile = jnp.where(is_live, near_features[source_index], jnp.zeros((), jnp.bfloat16))
        offset, radial, pair_basis = build_basis(
            own_points[tile_index], near_points[source_index], decay_rates
        )
        flat_basis = pair_basis.reshape(atom_count * basis_count, atom_count).astype(jnp.bfloat16)
        contribution = jnp.dot(flat_basis, near_tile, preferred_element_type=jnp.float32)
        return lax.dynamic_update_index_in_dim(
            summed, summed[tile_index] + contribution, tile_index, 0
        )

    summed = lax.fori_loop(
        0,
        pair_count,
        forward_pair,
        jnp.zeros((tile_count, atom_count * basis_count, channel_count), jnp.float32),
    )
    scaled_sum = summed.reshape(tile_count, atom_count, radial_count, 4, channel_count) * scaling
    scalar_part = scaled_sum[:, :, :, 0, :]
    vector_norm = jnp.sum(scaled_sum[:, :, :, 1:, :] * scaled_sum[:, :, :, 1:, :], axis=3)
    invariant = (
        jnp.concatenate([scalar_part, vector_norm], axis=2)
        .reshape(tile_count * atom_count, 2 * radial_count * channel_count)
        .astype(jnp.bfloat16)
    )
    preact = jnp.dot(invariant, mixing, preferred_element_type=jnp.float32)
    sigmoid_value = jax.nn.sigmoid(preact)
    grad_pre = (
        own_valid.reshape(-1, 1)
        * readout[None, :]
        * sigmoid_value
        * (1.0 + preact * (1.0 - sigmoid_value))
    ).astype(jnp.bfloat16)
    grad_invariant = lax.dot_general(
        grad_pre, mixing, (((1,), (1,)), ((), ())), preferred_element_type=jnp.float32
    )
    grad_invariant = grad_invariant.reshape(tile_count, atom_count, 2, radial_count, channel_count)
    grad_sum = (
        jnp.concatenate(
            [
                grad_invariant[:, :, 0, :, None, :],
                2.0 * scaled_sum[:, :, :, 1:, :] * grad_invariant[:, :, 1, :, None, :],
            ],
            axis=3,
        )
        * scaling
    )
    grad_sum = grad_sum.reshape(tile_count, atom_count * basis_count, channel_count).astype(
        jnp.bfloat16
    )

    def backward_pair(pair_index, state_pair):
        own_force, ghost_sum = state_pair
        tile_index, source_index, is_live, active = locate(pair_index)
        near_tile = jnp.where(is_live, near_features[source_index], jnp.zeros((), jnp.bfloat16))
        offset, radial, pair_basis = build_basis(
            own_points[tile_index], near_points[source_index], decay_rates
        )
        flat_basis = pair_basis.reshape(atom_count * basis_count, atom_count).astype(jnp.bfloat16)
        seed_rows = grad_sum[tile_index]
        grad_basis = lax.dot_general(
            seed_rows, near_tile, (((1,), (1,)), ((), ())), preferred_element_type=jnp.float32
        )
        grad_basis = grad_basis.reshape(atom_count, radial_count, 4, atom_count)
        grad_near = lax.dot_general(
            flat_basis, seed_rows, (((0,), (0,)), ((), ())), preferred_element_type=jnp.float32
        )
        inner_term = grad_basis[:, :, 0, :] + jnp.sum(
            grad_basis[:, :, 1:, :] * offset[:, None, :, :], axis=2
        )
        pair_force = jnp.sum(
            radial[:, :, None, :]
            * (
                grad_basis[:, :, 1:, :]
                - 2.0
                * decay_rates[None, :, None, None]
                * offset[:, None, :, :]
                * inner_term[:, :, None, :]
            ),
            axis=1,
        )
        own_part = jnp.transpose(jnp.sum(pair_force, axis=2))
        ghost_part = jnp.concatenate(
            [-jnp.sum(pair_force, axis=0).reshape(-1), grad_near.reshape(-1)]
        ) * is_live.astype(jnp.float32)
        own_part, ghost_part = (own_part, ghost_part)
        own_force = lax.dynamic_update_index_in_dim(
            own_force, own_force[tile_index] + own_part, tile_index, 0
        )
        ghost_sum = lax.dynamic_update_index_in_dim(
            ghost_sum, ghost_sum[source_index] + ghost_part, source_index, 0
        )
        return (own_force, ghost_sum)

    start_pair = (
        jnp.zeros((tile_count, 3, atom_count), jnp.float32),
        jnp.zeros((27 * tile_count, row_width), jnp.float32),
    )
    return lax.fori_loop(0, pair_count, backward_pair, start_pair)


def fold_plane(buffer, axis_dim, sender):
    lower_plane = lax.slice_in_dim(buffer, 0, 1, axis=axis_dim)
    middle_plane = lax.slice_in_dim(buffer, 1, 2, axis=axis_dim)
    upper_plane = lax.slice_in_dim(buffer, 2, 3, axis=axis_dim)
    result = middle_plane
    for toward in (1, -1):
        result = result + sender(upper_plane if toward == 1 else lower_plane, toward)
    return result


def body(positions, features, counts, neighbours, mix_weight, readout, radial_rates):
    tile_count = positions.shape[3]
    atom_count = positions.shape[5]
    channel_count = features.shape[5]
    row_width = (3 + channel_count) * atom_count
    own_counts = counts.reshape(tile_count)
    is_valid = lax.broadcasted_iota(jnp.int32, (tile_count, atom_count), 1) < own_counts[:, None]
    valid_float = is_valid.astype(jnp.float32)
    masked = jnp.where(
        is_valid.reshape(1, 1, 1, tile_count, atom_count, 1), features, jnp.zeros((), jnp.bfloat16)
    )
    near_points = extended(positions, (("gx", 0), ("gy", 1), ("gz", 2)), 1)
    near_features = extended(masked, (("gx", 0), ("gy", 1), ("gz", 2)), 1)
    near_points = near_points.reshape(27 * tile_count, 3, atom_count)
    near_features = near_features.reshape(27 * tile_count, atom_count, channel_count)
    own_force, ghost_sum = device_terms(
        positions.reshape(tile_count, 3, atom_count),
        valid_float,
        own_counts,
        near_points,
        near_features,
        neighbours.reshape(tile_count, -1),
        mix_weight,
        readout,
        radial_rates,
    )
    buffer = ghost_sum.reshape(3, 3, 3, tile_count, row_width)
    buffer = fold_plane(buffer, 0, lambda values, toward: from_behind(values, "gx", toward))
    buffer = fold_plane(buffer, 1, lambda values, toward: from_behind(values, "gy", toward))
    buffer = fold_plane(buffer, 2, lambda values, toward: from_behind(values, "gz", toward))
    center = buffer.reshape(tile_count, row_width)
    forces = own_force + center[:, : 3 * atom_count].reshape(tile_count, 3, atom_count)
    feature_grads = (
        center[:, 3 * atom_count :].reshape(tile_count, atom_count, channel_count)
        * valid_float[:, :, None]
    )
    return (
        forces.reshape(1, 1, 1, tile_count, 3, atom_count),
        feature_grads.reshape(1, 1, 1, tile_count, atom_count, channel_count),
    )


def solution(mesh):
    in_specs = (
        P("gx", "gy", "gz", None, None, None),
        P("gx", "gy", "gz", None, None, None),
        P("gx", "gy", "gz", None),
        P("gx", "gy", "gz", None, None),
        P(),
        P(),
        P(),
    )
    out_specs = (P("gx", "gy", "gz", None, None, None), P("gx", "gy", "gz", None, None, None))
    return jax.shard_map(body, mesh=mesh, in_specs=in_specs, out_specs=out_specs, check_vma=False)
```

profile of v0, /device:TPU:0, one launch (start us, length us, event | category | flops | bytes accessed | tf_op | source)
XLA Modules:
  0.0 319.8 jit_solution(5944236287602942780)
XLA Ops:
  3.7 3.0 collective-permute-start.6
  8.9 5.6 %collective-permute-start.8 = (bf16[3,1,1,2,128,128]{5,4,3,2,1,0:T(8,128)(2,1)S(1)}, bf16[3,1,1,2,128,128]{5,4,3,2,1,0:T(8,128)(2,1)S(1)}, u32[]{:S(2)}, u32[]{:S(2)}) collective-permute-start(bf16[3,1,1,2,128,128]{5,4,3,2,1,0:T(8,128)(2,1)S(1)} %pad_maximum_fusion.5), channel_id=1, source_target_pairs={{0,4},{4,8},{8,12},{1,5},{5,9},{9,13},{2,6},{6,10},{10,14},{3,7},{... | collective-permute-start | bytes 589832 | tf_op jit(solution)/shard_map/ppermute | solution.py:12
  20.6 4.6 %collective-permute-start.10 = (bf16[3,3,1,2,128,128]{5,4,3,2,1,0:T(8,128)(2,1)S(1)}, bf16[3,3,1,2,128,128]{5,4,3,2,1,0:T(8,128)(2,1)S(1)}, u32[]{:S(2)}, u32[]{:S(2)}) collective-permute-start(bf16[3,3,1,2,128,128]{5,4,3,2,1,0:T(8,128)(2,1)S(1)} %pad_maximum_fusion.3), channel_id=1, source_target_pairs={{0,1},{1,2},{2,3},{4,5},{5,6},{6,7},{8,9},{9,10},{10,11},{12,13},{... | collective-permute-start | bytes 1769480 | tf_op jit(solution)/shard_map/ppermute | solution.py:12
  27.2 5.0 %collective-permute-start.2 = (f32[3,1,1,2,3,128]{5,3,4,2,1,0:T(2,128)S(1)}, f32[3,1,1,2,3,128]{5,3,4,2,1,0:T(2,128)S(1)}, u32[]{:S(2)}, u32[]{:S(2)}) collective-permute-start(f32[3,1,1,2,3,128]{5,3,4,2,1,0:T(2,128)S(1)} %constant_dynamic-update-slice_fusion), channel_id=1, source_target_pairs={{0,4},{4,8},{8,12},{1,5},{5,9},{9,13},{2,6},{6,10},{10,14},{3,7},{... | collective-permute-start | bytes 27656 | tf_op jit(solution)/shard_map/ppermute | solution.py:12
  34.9 5.0 %collective-permute-start.4 = (f32[3,3,1,2,3,128]{5,3,4,2,1,0:T(2,128)S(1)}, f32[3,3,1,2,3,128]{5,3,4,2,1,0:T(2,128)S(1)}, u32[]{:S(2)}, u32[]{:S(2)}) collective-permute-start(f32[3,3,1,2,3,128]{5,3,4,2,1,0:T(2,128)S(1)} %pad_maximum_fusion.7), channel_id=1, source_target_pairs={{0,1},{1,2},{2,3},{4,5},{5,6},{6,7},{8,9},{9,10},{10,11},{12,13},{... | collective-permute-start | bytes 82952 | tf_op jit(solution)/shard_map/ppermute | solution.py:12
  40.0 9.8 %collective-permute-done.5 = f32[3,3,1,2,3,128]{5,3,4,2,1,0:T(2,128)S(1)} collective-permute-done((f32[3,3,1,2,3,128]{5,3,4,2,1,0:T(2,128)S(1)}, f32[3,3,1,2,3,128]{5,3,4,2,1,0:T(2,128)S(1)}, u32[]{:S(2)}, u32[]{:S(2)}) %collective-permute-start.5) | collective-permute-done | bytes 27680 | tf_op jit(solution)/shard_map/ppermute | solution.py:15
  51.9 71.7 %while.32 = (s32[]{:T(128)}, f32[2,2048,128]{2,1,0:T(8,128)S(1)}, f32[1,4,1]{1,2,0:T(1,128)S(1)}, s32[2,8]{1,0:T(2,128)S(1)}, f32[54,3,128]{2,1,0:T(4,128)S(1)},...) while((s32[]{:T(128)}, f32[2,2048,128]{2,1,0:T(8,128)S(1)}, ...), condition=%wide.region_2.3_spmd, body=%wide.region_0.2_spmd.sunk | while | flops 69156888 | bytes 8104349 | solution.py:78
  133.9 136.2 %while.33 = (s32[]{:T(128)}, f32[2,3,128]{2,0,1:T(2,128)S(1)}, f32[54,16768]{1,0:T(8,128)}, f32[1,4,1]{1,2,0:T(1,128)S(1)}, s32[2,8]{1,0:T(2,128)S(1)}, /*index=...) while((s32[]{:T(128)}, f32[2,3,128]{2,0,1:T(2,128)S(1)}, ...), condition=%wide.region_9.10_spmd, body=%wide.region_4.9_spmd.sunk | while | flops 136840352 | bytes 10953210 | solution.py:165
  139.9 2.6 dynamic_update_slice.39
  148.4 2.6 dynamic_update_slice.39
  156.9 2.6 dynamic_update_slice.39
  165.4 2.6 dynamic_update_slice.39
  173.9 2.6 dynamic_update_slice.39
  182.4 2.6 dynamic_update_slice.39
  191.0 2.6 dynamic_update_slice.39
  199.5 2.6 dynamic_update_slice.39
  208.0 2.6 dynamic_update_slice.39
  216.5 2.6 dynamic_update_slice.39
  225.0 2.6 dynamic_update_slice.39
  233.5 2.6 dynamic_update_slice.39
  242.0 2.6 dynamic_update_slice.39
  250.5 2.6 dynamic_update_slice.39
  259.0 2.6 dynamic_update_slice.39
  267.6 2.6 dynamic_update_slice.39
  270.1 4.1 %fusion.47 = (f32[18,16768]{1,0:T(8,128)}, f32[18,16768]{1,0:T(8,128)S(1)}, f32[18,16768]{1,0:T(8,128)S(1)}) fusion(f32[54,16768]{1,0:T(8,128)} %get-tuple-element.415), kind=kLoop, calls=%fused_computation.99 | loop fusion | bytes 7243776 | tf_op jit(solution)/shard_map/slice | solution.py:171
  274.2 2.9 slice.85
  280.2 5.1 %collective-permute-start.12 = (f32[1,3,3,2,16768]{4,3,2,1,0:T(2,128)}, f32[1,3,3,2,16768]{4,3,2,1,0:T(2,128)}, u32[]{:S(2)}, u32[]{:S(2)}) collective-permute-start(f32[1,3,3,2,16768]{4,3,2,1,0:T(2,128)} %slice.85), channel_id=1, source_target_pairs={{0,16},{1,17},{2,18},{3,19},{4,20},{5,21},{6,22},{7,23},{8,24},{9,... | collective-permute-start | bytes 3621896 | tf_op jit(solution)/shard_map/ppermute | solution.py:23
  289.7 4.0 %collective-permute-start.14 = (f32[1,1,3,2,16768]{4,3,2,1,0:T(2,128)S(1)}, f32[1,1,3,2,16768]{4,3,2,1,0:T(2,128)S(1)}, u32[]{:S(2)}, u32[]{:S(2)}) collective-permute-start(f32[1,1,3,2,16768]{4,3,2,1,0:T(2,128)S(1)} %get-tuple-element.464), channel_id=1, source_target_pairs={{0,4},{4,8},{8,12},{1,5},{5,9},{9,13},{2,6},{6,10},{10,14},{3,7},{... | collective-permute-start | bytes 1207304 | tf_op jit(solution)/shard_map/ppermute | solution.py:23
  295.0 7.8 %collective-permute-done.14 = f32[1,1,3,2,16768]{4,3,2,1,0:T(2,128)S(1)} collective-permute-done((f32[1,1,3,2,16768]{4,3,2,1,0:T(2,128)S(1)}, f32[1,1,3,2,16768]{4,3,2,1,0:T(2,128)S(1)}, u32[]{:S(2)}, u32[]{:S(2)}) %collective-permute-start.14) | collective-permute-done | bytes 402464 | tf_op jit(solution)/shard_map/ppermute | solution.py:23
  302.7 4.1 %collective-permute-done.15 = f32[1,1,3,2,16768]{4,3,2,1,0:T(2,128)S(1)} collective-permute-done((f32[1,1,3,2,16768]{4,3,2,1,0:T(2,128)S(1)}, f32[1,1,3,2,16768]{4,3,2,1,0:T(2,128)S(1)}, u32[]{:S(2)}, u32[]{:S(2)}) %collective-permute-start.15) | collective-permute-done | bytes 402464 | tf_op jit(solution)/shard_map/ppermute | solution.py:23
  307.3 4.2 %collective-permute-start.16 = (f32[1,1,1,2,16768]{4,3,2,1,0:T(2,128)S(1)}, f32[1,1,1,2,16768]{4,3,2,1,0:T(2,128)S(1)}, u32[]{:S(2)}, u32[]{:S(2)}) collective-permute-start(f32[1,1,1,2,16768]{4,3,2,1,0:T(2,128)S(1)} %get-tuple-element.468), channel_id=1, source_target_pairs={{0,1},{1,2},{2,3},{4,5},{5,6},{6,7},{8,9},{9,10},{10,11},{12,13},{... | collective-permute-start | bytes 402440 | tf_op jit(solution)/shard_map/ppermute | solution.py:23
  314.0 4.4 %collective-permute-done.17 = f32[1,1,1,2,16768]{4,3,2,1,0:T(2,128)S(1)} collective-permute-done((f32[1,1,1,2,16768]{4,3,2,1,0:T(2,128)S(1)}, f32[1,1,1,2,16768]{4,3,2,1,0:T(2,128)S(1)}, u32[]{:S(2)}, u32[]{:S(2)}) %collective-permute-start.17) | collective-permute-done | bytes 134176 | tf_op jit(solution)/shard_map/ppermute | solution.py:23
  (587 shorter events, 165.6 us)
Async XLA Ops:
  0.6 125.8 %copy-start = (bf16[1024,128]{1,0:T(8,128)(2,1)S(1)}, bf16[1024,128]{1,0:T(8,128)(2,1)}, u32[]{:S(2)}) copy-start(bf16[1024,128]{1,0:T(8,128)(2,1)} %param.15) | copy-start | bytes 786436
  0.6 39.3 %copy-start.4 = (f32[1,1,1,2,3,128]{5,3,4,2,1,0:T(2,128)S(1)}, f32[1,1,1,2,3,128]{5,3,4,2,1,0:T(2,128)}, u32[]{:S(2)}) copy-start(f32[1,1,1,2,3,128]{5,3,4,2,1,0:T(2,128)} %param.11) | copy-start | bytes 9220
  0.7 39.3 %copy-start.6 = (f32[4]{0:T(128)S(1)}, f32[4]{0:T(128)}, u32[]{:S(2)}) copy-start(f32[4]{0:T(128)} %param.17) | copy-start | bytes 52
  2.4 4.3 %collective-permute-start.7 = (bf16[1,1,1,2,128,128]{5,4,3,2,1,0:T(8,128)(2,1)S(1)}, bf16[1,1,1,2,128,128]{5,4,3,2,1,0:T(8,128)(2,1)S(1)}, u32[]{:S(2)}, u32[]{:S(2)}) collective-permute-start(bf16[1,1,1,2,128,128]{5,4,3,2,1,0:T(8,128)(2,1)S(1)} %broadcast_select_fusion), channel_id=1, source_target_pairs={{16,0},{17,1},{18,2},{19,3},{20,4},{21,5},{22,6},{23,7},{24,8},{25... | collective-permute-start | bytes 196616 | tf_op jit(solution)/shard_map/ppermute | solution.py:15
  3.7 3.9 %collective-permute-start.6 = (bf16[1,1,1,2,128,128]{5,4,3,2,1,0:T(8,128)(2,1)S(1)}, bf16[1,1,1,2,128,128]{5,4,3,2,1,0:T(8,128)(2,1)S(1)}, u32[]{:S(2)}, u32[]{:S(2)}) collective-permute-start(bf16[1,1,1,2,128,128]{5,4,3,2,1,0:T(8,128)(2,1)S(1)} %broadcast_select_fusion), channel_id=1, source_target_pairs={{0,16},{1,17},{2,18},{3,19},{4,20},{5,21},{6,22},{7,23},{8,24},{9,... | collective-permute-start | bytes 196616 | tf_op jit(solution)/shard_map/ppermute | solution.py:12
  7.6 10.4 %collective-permute-start.9 = (bf16[3,1,1,2,128,128]{5,4,3,2,1,0:T(8,128)(2,1)S(1)}, bf16[3,1,1,2,128,128]{5,4,3,2,1,0:T(8,128)(2,1)S(1)}, u32[]{:S(2)}, u32[]{:S(2)}) collective-permute-start(bf16[3,1,1,2,128,128]{5,4,3,2,1,0:T(8,128)(2,1)S(1)} %pad_maximum_fusion.5), channel_id=1, source_target_pairs={{4,0},{8,4},{12,8},{5,1},{9,5},{13,9},{6,2},{10,6},{14,10},{7,3},{... | collective-permute-start | bytes 589832 | tf_op jit(solution)/shard_map/ppermute | solution.py:15
  8.9 10.3 %collective-permute-start.8 = (bf16[3,1,1,2,128,128]{5,4,3,2,1,0:T(8,128)(2,1)S(1)}, bf16[3,1,1,2,128,128]{5,4,3,2,1,0:T(8,128)(2,1)S(1)}, u32[]{:S(2)}, u32[]{:S(2)}) collective-permute-start(bf16[3,1,1,2,128,128]{5,4,3,2,1,0:T(8,128)(2,1)S(1)} %pad_maximum_fusion.5), channel_id=1, source_target_pairs={{0,4},{4,8},{8,12},{1,5},{5,9},{9,13},{2,6},{6,10},{10,14},{3,7},{... | collective-permute-start | bytes 589832 | tf_op jit(solution)/shard_map/ppermute | solution.py:12
  14.5 3.3 %collective-permute-start = (f32[1,1,1,2,3,128]{5,3,4,2,1,0:T(2,128)}, f32[1,1,1,2,3,128]{5,3,4,2,1,0:T(2,128)S(1)}, u32[]{:S(2)}, u32[]{:S(2)}) collective-permute-start(f32[1,1,1,2,3,128]{5,3,4,2,1,0:T(2,128)} %param.11), channel_id=1, source_target_pairs={{0,16},{1,17},{2,18},{3,19},{4,20},{5,21},{6,22},{7,23},{8,24},{9,... | collective-permute-start | bytes 9224 | tf_op jit(solution)/shard_map/ppermute | solution.py:12
  16.5 9.3 %collective-permute-start.1 = (f32[1,1,1,2,3,128]{5,3,4,2,1,0:T(2,128)}, f32[1,1,1,2,3,128]{5,3,4,2,1,0:T(2,128)S(1)}, u32[]{:S(2)}, u32[]{:S(2)}) collective-permute-start(f32[1,1,1,2,3,128]{5,3,4,2,1,0:T(2,128)} %param.11), channel_id=1, source_target_pairs={{16,0},{17,1},{18,2},{19,3},{20,4},{21,5},{22,6},{23,7},{24,8},{25... | collective-permute-start | bytes 9224 | tf_op jit(solution)/shard_map/ppermute | solution.py:15
  19.3 30.6 %collective-permute-start.11 = (bf16[3,3,1,2,128,128]{5,4,3,2,1,0:T(8,128)(2,1)S(1)}, bf16[3,3,1,2,128,128]{5,4,3,2,1,0:T(8,128)(2,1)S(1)}, u32[]{:S(2)}, u32[]{:S(2)}) collective-permute-start(bf16[3,3,1,2,128,128]{5,4,3,2,1,0:T(8,128)(2,1)S(1)} %pad_maximum_fusion.3), channel_id=1, source_target_pairs={{1,0},{2,1},{3,2},{5,4},{6,5},{7,6},{9,8},{10,9},{11,10},{13,12},{... | collective-permute-start | bytes 1769480 | tf_op jit(solution)/shard_map/ppermute | solution.py:15
  20.6 29.3 %collective-permute-start.10 = (bf16[3,3,1,2,128,128]{5,4,3,2,1,0:T(8,128)(2,1)S(1)}, bf16[3,3,1,2,128,128]{5,4,3,2,1,0:T(8,128)(2,1)S(1)}, u32[]{:S(2)}, u32[]{:S(2)}) collective-permute-start(bf16[3,3,1,2,128,128]{5,4,3,2,1,0:T(8,128)(2,1)S(1)} %pad_maximum_fusion.3), channel_id=1, source_target_pairs={{0,1},{1,2},{2,3},{4,5},{5,6},{6,7},{8,9},{9,10},{10,11},{12,13},{... | collective-permute-start | bytes 1769480 | tf_op jit(solution)/shard_map/ppermute | solution.py:12
  25.9 6.3 %collective-permute-start.3 = (f32[3,1,1,2,3,128]{5,3,4,2,1,0:T(2,128)S(1)}, f32[3,1,1,2,3,128]{5,3,4,2,1,0:T(2,128)S(1)}, u32[]{:S(2)}, u32[]{:S(2)}) collective-permute-start(f32[3,1,1,2,3,128]{5,3,4,2,1,0:T(2,128)S(1)} %constant_dynamic-update-slice_fusion), channel_id=1, source_target_pairs={{4,0},{8,4},{12,8},{5,1},{9,5},{13,9},{6,2},{10,6},{14,10},{7,3},{... | collective-permute-start | bytes 27656 | tf_op jit(solution)/shard_map/ppermute | solution.py:15
  27.2 6.4 %collective-permute-start.2 = (f32[3,1,1,2,3,128]{5,3,4,2,1,0:T(2,128)S(1)}, f32[3,1,1,2,3,128]{5,3,4,2,1,0:T(2,128)S(1)}, u32[]{:S(2)}, u32[]{:S(2)}) collective-permute-start(f32[3,1,1,2,3,128]{5,3,4,2,1,0:T(2,128)S(1)} %constant_dynamic-update-slice_fusion), channel_id=1, source_target_pairs={{0,4},{4,8},{8,12},{1,5},{5,9},{9,13},{2,6},{6,10},{10,14},{3,7},{... | collective-permute-start | bytes 27656 | tf_op jit(solution)/shard_map/ppermute | solution.py:12
  33.6 16.2 %collective-permute-start.5 = (f32[3,3,1,2,3,128]{5,3,4,2,1,0:T(2,128)S(1)}, f32[3,3,1,2,3,128]{5,3,4,2,1,0:T(2,128)S(1)}, u32[]{:S(2)}, u32[]{:S(2)}) collective-permute-start(f32[3,3,1,2,3,128]{5,3,4,2,1,0:T(2,128)S(1)} %pad_maximum_fusion.7), channel_id=1, source_target_pairs={{1,0},{2,1},{3,2},{5,4},{6,5},{7,6},{9,8},{10,9},{11,10},{13,12},{... | collective-permute-start | bytes 82952 | tf_op jit(solution)/shard_map/ppermute | solution.py:15
  34.9 14.9 %collective-permute-start.4 = (f32[3,3,1,2,3,128]{5,3,4,2,1,0:T(2,128)S(1)}, f32[3,3,1,2,3,128]{5,3,4,2,1,0:T(2,128)S(1)}, u32[]{:S(2)}, u32[]{:S(2)}) collective-permute-start(f32[3,3,1,2,3,128]{5,3,4,2,1,0:T(2,128)S(1)} %pad_maximum_fusion.7), channel_id=1, source_target_pairs={{0,1},{1,2},{2,3},{4,5},{5,6},{6,7},{8,9},{9,10},{10,11},{12,13},{... | collective-permute-start | bytes 82952 | tf_op jit(solution)/shard_map/ppermute | solution.py:12
  51.2 0.7 copy-start.3
  123.8 2.1 copy-start.1
  125.5 1.0 copy-start.5
  127.9 2.1 copy-start.2
  278.9 7.1 %collective-permute-start.13 = (f32[1,3,3,2,16768]{4,3,2,1,0:T(2,128)}, f32[1,3,3,2,16768]{4,3,2,1,0:T(2,128)}, u32[]{:S(2)}, u32[]{:S(2)}) collective-permute-start(f32[1,3,3,2,16768]{4,3,2,1,0:T(2,128)} %slice.87), channel_id=1, source_target_pairs={{16,0},{17,1},{18,2},{19,3},{20,4},{21,5},{22,6},{23,7},{24,8},{25... | collective-permute-start | bytes 3621896 | tf_op jit(solution)/shard_map/ppermute | solution.py:23
  280.2 6.9 %collective-permute-start.12 = (f32[1,3,3,2,16768]{4,3,2,1,0:T(2,128)}, f32[1,3,3,2,16768]{4,3,2,1,0:T(2,128)}, u32[]{:S(2)}, u32[]{:S(2)}) collective-permute-start(f32[1,3,3,2,16768]{4,3,2,1,0:T(2,128)} %slice.85), channel_id=1, source_target_pairs={{0,16},{1,17},{2,18},{3,19},{4,20},{5,21},{6,22},{7,23},{8,24},{9,... | collective-permute-start | bytes 3621896 | tf_op jit(solution)/shard_map/ppermute | solution.py:23
  289.7 13.1 %collective-permute-start.14 = (f32[1,1,3,2,16768]{4,3,2,1,0:T(2,128)S(1)}, f32[1,1,3,2,16768]{4,3,2,1,0:T(2,128)S(1)}, u32[]{:S(2)}, u32[]{:S(2)}) collective-permute-start(f32[1,1,3,2,16768]{4,3,2,1,0:T(2,128)S(1)} %get-tuple-element.464), channel_id=1, source_target_pairs={{0,4},{4,8},{8,12},{1,5},{5,9},{9,13},{2,6},{6,10},{10,14},{3,7},{... | collective-permute-start | bytes 1207304 | tf_op jit(solution)/shard_map/ppermute | solution.py:23
  293.7 13.2 %collective-permute-start.15 = (f32[1,1,3,2,16768]{4,3,2,1,0:T(2,128)S(1)}, f32[1,1,3,2,16768]{4,3,2,1,0:T(2,128)S(1)}, u32[]{:S(2)}, u32[]{:S(2)}) collective-permute-start(f32[1,1,3,2,16768]{4,3,2,1,0:T(2,128)S(1)} %get-tuple-element.465), channel_id=1, source_target_pairs={{4,0},{8,4},{12,8},{5,1},{9,5},{13,9},{6,2},{10,6},{14,10},{7,3},{... | collective-permute-start | bytes 1207304 | tf_op jit(solution)/shard_map/ppermute | solution.py:23
  307.3 6.7 %collective-permute-start.16 = (f32[1,1,1,2,16768]{4,3,2,1,0:T(2,128)S(1)}, f32[1,1,1,2,16768]{4,3,2,1,0:T(2,128)S(1)}, u32[]{:S(2)}, u32[]{:S(2)}) collective-permute-start(f32[1,1,1,2,16768]{4,3,2,1,0:T(2,128)S(1)} %get-tuple-element.468), channel_id=1, source_target_pairs={{0,1},{1,2},{2,3},{4,5},{5,6},{6,7},{8,9},{9,10},{10,11},{12,13},{... | collective-permute-start | bytes 402440 | tf_op jit(solution)/shard_map/ppermute | solution.py:23
  311.5 6.9 %collective-permute-start.17 = (f32[1,1,1,2,16768]{4,3,2,1,0:T(2,128)S(1)}, f32[1,1,1,2,16768]{4,3,2,1,0:T(2,128)S(1)}, u32[]{:S(2)}, u32[]{:S(2)}) collective-permute-start(f32[1,1,1,2,16768]{4,3,2,1,0:T(2,128)S(1)} %get-tuple-element.469), channel_id=1, source_target_pairs={{1,0},{2,1},{3,2},{5,4},{6,5},{7,6},{9,8},{10,9},{11,10},{13,12},{... | collective-permute-start | bytes 402440 | tf_op jit(solution)/shard_map/ppermute | solution.py:23
where the time goes:
time: 325 us; the launch traced here: 320 us
  local copies, waits for them, and re-layouts  90.9 us (28%)
  other arithmetic  62.8 us (19%)
  starting transfers between devices  50.1 us (15%)
  loops' own time  42 us (13%)
  matrix products  40.9 us (13%)
  waiting for transfers between devices  31.9 us (10%)
    dynamic_update_slice x16, local copies, waits for them, and re-layouts, backward_pair(): lax.dynamic_update_index_in_dim(ghost_sum, ghost_sum[source_index] + ghos...  41.4 us
    ppermute x6, starting transfers between devices, extended(): lax.ppermute(lax.slice_in_dim(block, block.shape[dim] - width, None, axis...  25.3 us
    another operation x1, loops' own time, device_terms(): return lax.fori_loop(0, pair_count, backward_pair, start_pair)  22.4 us
    another operation x1, loops' own time, device_terms(): lax.fori_loop(0, pair_count, forward_pair, jnp.zeros((tile_count, atom_co...  19.6 us
    dynamic_slice x32, local copies, waits for them, and re-layouts, locate(): target = neighbour_rows[tile_index, slot_index]  18.7 us
    ppermute x6, waiting for transfers between devices, from_behind(): return lax.ppermute(block, axis, route)  18.6 us
    add x16, other arithmetic, backward_pair(): ghost_sum[source_index] + ghost_part  18.4 us
    dot_general x16, matrix products, backward_pair(): lax.dot_general(seed_rows, near_tile, (((1,), (1,)), ((), ())), preferred...  17.2 us
  transfers between devices with their start and end apart: 18, of which 10 were waited for; matrix products, arithmetic and copies ran while one was open for 0% of the time, Pallas kernels for 0%

commit v1 on v0

v1 whole, which is shorter than its diff:
```python
import functools

import jax
import jax.numpy as jnp
from jax import lax
from jax.experimental import pallas as pl
from jax.experimental.pallas import tpu as pltpu
from jax.sharding import PartitionSpec as P

ROWS = 32
EXTRA = 8
NT = (((1,), (1,)), ((), ()))


def swaps(axis):
    count = lax.axis_size(axis)
    result = []
    for first in (0, 1):
        pairs = [(i, i + 1) for i in range(first, count - 1, 2)]
        if pairs:
            result.append(pairs + [(b, a) for a, b in pairs])
    return result


def place(step, axis):
    side = jnp.where((step == 1) == (lax.axis_index(axis) % 2 == 0), 1, 2)
    return jnp.minimum(jnp.where(step == 0, 0, side), len(swaps(axis)))


def pack_kernel(counts_ref, features_ref, points_ref, packed_ref, extra_ref):
    tiles, atoms, _ = features_ref.shape
    for t in range(tiles):
        count = counts_ref[t]
        rows = lax.broadcasted_iota(jnp.int32, features_ref.shape[1:], 0)
        values = features_ref[t].astype(jnp.float32)
        packed_ref[t, :atoms] = jnp.where(rows < count, values, 0.0).astype(jnp.bfloat16)
        rest = points_ref[t]
        extra_ref[...] = jnp.zeros_like(extra_ref)
        for term in range(3):
            part = rest.astype(jnp.bfloat16).astype(jnp.float32)
            extra_ref[3 * term : 3 * term + 3] = part
            rest = rest - part
        packed_ref[t, atoms:] = extra_ref[...].astype(jnp.bfloat16)


def main_kernel(
    planes,
    slots,
    counts_ref,
    index_ref,
    live_ref,
    rates_ref,
    points_ref,
    mixing_ref,
    readout_ref,
    *refs,
):
    plane_refs = refs[:planes]
    ghost_refs = refs[planes : 2 * planes]
    (
        near_ref,
        own_ref,
        basis_ref,
        radial_ref,
        pair_features_ref,
        sum_ref,
        seed_ref,
        seed_t_ref,
        grad_ref,
        near_grad_ref,
        near_force_ref,
        own_force_ref,
        ghost_ref,
        in_sems,
        out_sems,
    ) = refs[2 * planes :]
    tiles, _, atoms = points_ref.shape
    channels = readout_ref.shape[1]
    radials = rates_ref.shape[0]
    bases = 4 * radials
    chunk_rows = bases * ROWS
    couples = slots // 2
    plane_tiles = plane_refs[0].shape[0]
    scaling = (slots * atoms) ** (-0.5)

    loads = [
        pltpu.make_async_copy(
            plane_refs[k], near_ref.at[pl.ds(k * plane_tiles, plane_tiles)], in_sems.at[k]
        )
        for k in range(planes)
    ]
    for load in loads:
        load.start()

    for t in range(tiles):
        for m in range(3):
            line = points_ref[t, m : m + 1, :]
            own_ref[t, m] = jnp.transpose(jnp.broadcast_to(line, (atoms, atoms)))
    ghost_ref[...] = jnp.zeros_like(ghost_ref)
    own_force_ref[...] = jnp.zeros_like(own_force_ref)
    sum_ref[...] = jnp.zeros_like(sum_ref)

    for load in loads:
        load.wait()

    def near_points(tile):
        extra = near_ref[tile, atoms:, :].astype(jnp.float32)
        total = extra[0:3] + extra[3:6] + extra[6:9]
        return [total[m : m + 1, :] for m in range(3)]

    def members(t, couple):
        first = t * slots + 2 * couple
        return index_ref[first], index_ref[first + 1], 2 * couple + 1 < live_ref[t]

    rates = [rates_ref[r] for r in range(radials)]

    for t in range(tiles):
        count = counts_ref[t]
        chunks = (count + (ROWS - 1)) // ROWS
        active = jnp.where(count > 0, (live_ref[t] + 1) // 2, 0)

        def forward(couple, carry, t=t, chunks=chunks):
            one, two, both = members(t, couple)
            slot = t * couples + couple
            pair_features_ref[slot, :atoms] = near_ref[one, :atoms, :]
            second = near_ref[two, :atoms, :]
            pair_features_ref[slot, atoms:] = jnp.where(both, second, jnp.zeros_like(second))
            points = (near_points(one), near_points(two))

            def chunk_step(chunk, carry):
                start = pl.multiple_of(chunk * ROWS, ROWS)
                base = pl.multiple_of(chunk * chunk_rows, chunk_rows)
                for half in range(2):
                    lanes = slice(half * atoms, (half + 1) * atoms)
                    for sub in range(0, ROWS, 16):
                        offset = [
                            points[half][m] - own_ref[t, m, pl.ds(start + sub, 16), :]
                            for m in range(3)
                        ]
                        square = (
                            offset[0] * offset[0] + offset[1] * offset[1] + offset[2] * offset[2]
                        )
                        for r in range(radials):
                            radial = jnp.exp(-rates[r] * square)
                            radial_ref[slot, half, r, pl.ds(start + sub, 16), :] = radial
                            for m in range(4):
                                value = radial if m == 0 else radial * offset[m - 1]
                                row = base + (4 * r + m) * ROWS + sub
                                basis_ref[slot, pl.ds(row, 16), lanes] = value.astype(jnp.bfloat16)
                sum_ref[t, pl.ds(base, chunk_rows), :] += jnp.dot(
                    basis_ref[slot, pl.ds(base, chunk_rows), :],
                    pair_features_ref[slot],
                    preferred_element_type=jnp.float32,
                )
                return carry

            return lax.fori_loop(0, chunks, chunk_step, carry)

        lax.fori_loop(0, active, forward, 0)

        def middle(chunk, carry, t=t, count=count):
            base = pl.multiple_of(chunk * chunk_rows, chunk_rows)
            parts = []
            norms = []
            for r in range(radials):
                for m in range(4):
                    value = sum_ref[t, pl.ds(base + (4 * r + m) * ROWS, ROWS), :] * scaling
                    if m == 0:
                        parts.append(value)
                    elif m == 1:
                        norm = value * value
                    else:
                        norm = norm + value * value
                norms.append(norm)
            invariant = jnp.concatenate(parts + norms, axis=1).astype(jnp.bfloat16)
            preact = jnp.dot(invariant, mixing_ref[...], preferred_element_type=jnp.float32)
            sigmoid = jax.nn.sigmoid(preact)
            row = lax.broadcasted_iota(jnp.int32, (ROWS, channels), 0) + chunk * ROWS
            valid = (row < count).astype(jnp.float32)
            grad_pre = valid * readout_ref[...] * sigmoid * (1.0 + preact * (1.0 - sigmoid))
            grad = lax.dot_general(
                grad_pre.astype(jnp.bfloat16),
                mixing_ref[...],
                NT,
                preferred_element_type=jnp.float32,
            )
            for r in range(radials):
                scalar = grad[:, r * channels : (r + 1) * channels]
                square = grad[:, (radials + r) * channels : (radials + r + 1) * channels]
                for m in range(4):
                    row = base + (4 * r + m) * ROWS
                    if m == 0:
                        value = scalar * scaling
                    else:
                        value = sum_ref[t, pl.ds(row, ROWS), :] * scaling
                        value = 2.0 * value * square * scaling
                    value = value.astype(jnp.bfloat16)
                    seed_ref[t, pl.ds(row, ROWS), :] = value
            seed_t_ref[t, chunk] = jnp.transpose(seed_ref[t, pl.ds(base, chunk_rows), :])
            return carry

        lax.fori_loop(0, jnp.where(count > 0, chunks, 0), middle, 0)

        def backward(couple, carry, t=t, chunks=chunks):
            one, two, both = members(t, couple)
            slot = t * couples + couple
            points = (near_points(one), near_points(two))
            near_grad_ref[...] = jnp.zeros_like(near_grad_ref)
            near_force_ref[...] = jnp.zeros_like(near_force_ref)

            def chunk_step(chunk, carry):
                start = pl.multiple_of(chunk * ROWS, ROWS)
                base = pl.multiple_of(chunk * chunk_rows, chunk_rows)
                grad_ref[...] = lax.dot_general(
                    seed_ref[t, pl.ds(base, chunk_rows), :],
                    pair_features_ref[slot],
                    NT,
                    preferred_element_type=jnp.float32,
                )
                near_grad_ref[...] += jnp.dot(
                    seed_t_ref[t, chunk],
                    basis_ref[slot, pl.ds(base, chunk_rows), :],
                    preferred_element_type=jnp.float32,
                )
                for half in range(2):
                    lanes = slice(half * atoms, (half + 1) * atoms)
                    pulled = [None] * 3
                    for sub in range(0, ROWS, 8):
                        where = pl.ds(start + sub, 8)
                        offset = [points[half][m] - own_ref[t, m, where, :] for m in range(3)]
                        direct = [None] * 4
                        decayed = [None] * 4
                        for r in range(radials):
                            radial = radial_ref[slot, half, r, where, :]
                            steep = radial * (2.0 * rates[r])
                            for m in range(4):
                                row = (4 * r + m) * ROWS + sub
                                grad = grad_ref[row : row + 8, lanes]
                                if m > 0:
                                    part = radial * grad
                                    direct[m] = part if r == 0 else direct[m] + part
                                part = steep * grad
                                decayed[m] = part if r == 0 else decayed[m] + part
                        inner = decayed[0]
                        for m in range(3):
                            inner = inner + decayed[m + 1] * offset[m]
                        for m in range(3):
                            force = direct[m + 1] - offset[m] * inner
                            own_force_ref[t, m, where, :] += force
                            pulled[m] = force if sub == 0 else pulled[m] + force
                    for m in range(3):
                        near_force_ref[half, m] += pulled[m]
                return carry

            lax.fori_loop(0, chunks, chunk_step, 0)

            def give(half, tile):
                lanes = slice(half * atoms, (half + 1) * atoms)
                ghost_ref[tile, :channels, :] += near_grad_ref[:, lanes]
                for m in range(3):
                    ghost_ref[tile, channels + m : channels + m + 1, :] -= jnp.sum(
                        near_force_ref[half, m], axis=0, keepdims=True
                    )

            give(0, one)

            @pl.when(both)
            def _():
                give(1, two)

            return carry

        lax.fori_loop(0, active, backward, 0)
        for m in range(3):
            ghost_ref[t, channels + m : channels + m + 1, :] += jnp.sum(
                jnp.transpose(own_force_ref[t, m]), axis=0, keepdims=True
            )

    stores = [
        pltpu.make_async_copy(
            ghost_ref.at[pl.ds(k * plane_tiles, plane_tiles)], ghost_refs[k], out_sems.at[k]
        )
        for k in range(planes)
    ]
    for store in stores:
        store.start()
    for store in stores:
        store.wait()


def final_kernel(counts_ref, *refs):
    part_refs = refs[:-2]
    forces_ref, grads_ref = refs[-2:]
    tiles, channels, atoms = grads_ref.shape
    for t in range(tiles):
        total = part_refs[0][t]
        for part in part_refs[1:]:
            total = total + part[t]
        forces_ref[t] = total[channels : channels + 3]
        column = lax.broadcasted_iota(jnp.int32, (channels, atoms), 1)
        masked = jnp.where(column < counts_ref[t], total[:channels], 0.0)
        grads_ref[t] = jnp.transpose(masked)


def body(positions, features, counts, neighbours, mix_weight, readout, radial_rates):
    tiles, atoms = positions.shape[3], positions.shape[5]
    channels = features.shape[5]
    slots = neighbours.shape[4]
    radials = radial_rates.shape[0]
    vmem = pl.BlockSpec(memory_space=pltpu.VMEM)
    smem = pl.BlockSpec(memory_space=pltpu.SMEM)
    hbm = pl.BlockSpec(memory_space=pl.ANY)

    own_counts = counts.reshape(tiles)
    points = positions.reshape(tiles, 3, atoms)
    packed = pl.pallas_call(
        pack_kernel,
        out_shape=jax.ShapeDtypeStruct((tiles, atoms + 16, channels), jnp.bfloat16),
        in_specs=[smem, vmem, vmem],
        out_specs=vmem,
        scratch_shapes=[pltpu.VMEM((16, channels), jnp.float32)],
        name="pack",
    )(own_counts, features.reshape(tiles, atoms, channels), points)

    block = packed
    for axis in ("gz", "gy"):
        parts = [block] + [lax.ppermute(block, axis, pairs) for pairs in swaps(axis)]
        block = jnp.concatenate(parts, axis=0)
    planes = [block] + [lax.ppermute(block, "gx", pairs) for pairs in swaps("gx")]

    rows = neighbours.reshape(tiles, slots)
    live = jnp.sum((rows >= 0).astype(jnp.int32), axis=1)
    target = jnp.maximum(rows, 0)
    step = target // tiles
    spot = place(step // 9 - 1, "gx")
    spot = spot * (len(swaps("gy")) + 1) + place(step // 3 % 3 - 1, "gy")
    spot = spot * (len(swaps("gz")) + 1) + place(step % 3 - 1, "gz")
    index = spot * tiles + target % tiles
    if slots % 2:
        index = jnp.pad(index, ((0, 0), (0, 1)))
    even_slots = slots + slots % 2

    count = len(planes)
    plane_tiles = block.shape[0]
    total = count * plane_tiles
    couples = even_slots // 2
    bases = 4 * radials
    chunks = atoms // ROWS
    ghost_rows = channels + EXTRA
    ghosts = pl.pallas_call(
        functools.partial(main_kernel, count, even_slots),
        out_shape=[jax.ShapeDtypeStruct((plane_tiles, ghost_rows, atoms), jnp.float32)] * count,
        in_specs=[smem] * 4 + [vmem] * 3 + [hbm] * count,
        out_specs=[hbm] * count,
        scratch_shapes=[
            pltpu.VMEM((total, atoms + 16, channels), jnp.bfloat16),
            pltpu.VMEM((tiles, 3, atoms, atoms), jnp.float32),
            pltpu.VMEM((tiles * couples, bases * atoms, 2 * atoms), jnp.bfloat16),
            pltpu.VMEM((tiles * couples, 2, radials, atoms, atoms), jnp.float32),
            pltpu.VMEM((tiles * couples, 2 * atoms, channels), jnp.bfloat16),
            pltpu.VMEM((tiles, bases * atoms, channels), jnp.float32),
            pltpu.VMEM((tiles, bases * atoms, channels), jnp.bfloat16),
            pltpu.VMEM((tiles, chunks, channels, bases * ROWS), jnp.bfloat16),
            pltpu.VMEM((bases * ROWS, 2 * atoms), jnp.float32),
            pltpu.VMEM((channels, 2 * atoms), jnp.float32),
            pltpu.VMEM((2, 3, 8, atoms), jnp.float32),
            pltpu.VMEM((tiles, 3, atoms, atoms), jnp.float32),
            pltpu.VMEM((total, ghost_rows, atoms), jnp.float32),
            pltpu.SemaphoreType.DMA((count,)),
            pltpu.SemaphoreType.DMA((count,)),
        ],
        name="pairs",
    )(
        own_counts,
        index.reshape(-1),
        live,
        radial_rates,
        points,
        mix_weight,
        readout.reshape(1, channels),
        *planes,
    )

    folded = ghosts[0]
    for ghost, pairs in zip(ghosts[1:], swaps("gx")):
        folded = folded + lax.ppermute(ghost, "gx", pairs)
    sides = len(swaps("gy")) + 1
    folded = folded.reshape(sides, plane_tiles // sides, ghost_rows, atoms)
    total_part = folded[0]
    for k, pairs in enumerate(swaps("gy")):
        total_part = total_part + lax.ppermute(folded[k + 1], "gy", pairs)
    sides = len(swaps("gz")) + 1
    folded = total_part.reshape(sides, tiles, ghost_rows, atoms)
    parts = [folded[0]]
    for k, pairs in enumerate(swaps("gz")):
        parts.append(lax.ppermute(folded[k + 1], "gz", pairs))

    forces, grads = pl.pallas_call(
        final_kernel,
        out_shape=[
            jax.ShapeDtypeStruct((tiles, 3, atoms), jnp.float32),
            jax.ShapeDtypeStruct((tiles, channels, atoms), jnp.float32),
        ],
        in_specs=[smem] + [vmem] * len(parts),
        out_specs=[vmem, vmem],
        name="finish",
    )(own_counts, *parts)
    return (
        forces.reshape(1, 1, 1, tiles, 3, atoms),
        grads.reshape(1, 1, 1, tiles, atoms, channels),
    )


def solution(mesh):
    in_specs = (
        P("gx", "gy", "gz", None, None, None),
        P("gx", "gy", "gz", None, None, None),
        P("gx", "gy", "gz", None),
        P("gx", "gy", "gz", None, None),
        P(),
        P(),
        P(),
    )
    out_specs = (P("gx", "gy", "gz", None, None, None), P("gx", "gy", "gz", None, None, None))
    return jax.shard_map(body, mesh=mesh, in_specs=in_specs, out_specs=out_specs, check_vma=False)
```

time: 325 us -> 79 us (0.24); the launches traced: 320 us -> 77.6 us
  local copies, waits for them, and re-layouts: 90.9 us -> 6.06 us
  other arithmetic: 62.8 us -> 3.65 us
  loops' own time: 42 us -> 0 us
  matrix products: 40.9 us -> 0 us
  starting transfers between devices: 50.1 us -> 34.1 us
  Pallas kernels: 0 us -> 7.38 us
  waiting for transfers between devices: 31.9 us -> 25.7 us
    dynamic_update_slice x48 -> x0, local copies, waits for them, and re-layouts: 42.2 us -> none  [the longest x16 41.4 us: backward_pair(): lax.dynamic_update_index_in_dim(ghost_sum, ghost_sum[source_index] + ghos...]
    another operation x2 -> x0, loops' own time: 42 us -> none  [the longest x1 22.4 us: device_terms(): return lax.fori_loop(0, pair_count, backward_pair, start_pair)]
    dot_general x49 -> x0, matrix products: 40.9 us -> none  [the longest x16 17.2 us: backward_pair(): lax.dot_general(seed_rows, near_tile, (((1,), (1,)), ((), ())), preferred...]
    dynamic_slice x80 -> x0, local copies, waits for them, and re-layouts: 20.8 us -> none  [the longest x32 18.7 us: locate(): target = neighbour_rows[tile_index, slot_index]]
    add x18 -> x3, other arithmetic: 21.2 us -> 2.11 us  [the longest x1 1.48 us: body(): folded = folded + lax.ppermute(ghost, 'gx', pairs)]
    ppermute x18 -> x10, starting transfers between devices: 50.1 us -> 34.1 us  [the longest x2 14.9 us: body(): total_part = total_part + lax.ppermute(folded[k + 1], 'gy', pairs)]
    reduce_sum x65 -> x1, other arithmetic: 12.1 us -> 0.63 us  [body(): live = jnp.sum((rows >= 0).astype(jnp.int32), axis=1)]
    concatenate x38 -> x1, other arithmetic: 11.3 us -> 0.91 us  [body(): block = jnp.concatenate(parts, axis=0)]
  transfers between devices with their start and end apart: 18 -> 10, of which waited for: 10 -> 6; matrix products, arithmetic and copies ran while one was open for 0% -> 3% of each run, Pallas kernels for 0% -> 0%
where the time goes in v1:
time: 79 us; the launch traced here: 77.6 us
  starting transfers between devices  34.1 us (43%)
  waiting for transfers between devices  25.7 us (33%)
  Pallas kernels  7.38 us (9%)
  local copies, waits for them, and re-layouts  6.06 us (8%)
  other arithmetic  3.65 us (5%)
    ppermute x2, starting transfers between devices, body(): total_part = total_part + lax.ppermute(folded[k + 1], 'gy', pairs)  14.9 us
    ppermute x4, starting transfers between devices, body(): lax.ppermute(block, axis, pairs)  11.5 us
    ppermute x2, waiting for transfers between devices, body(): total_part = total_part + lax.ppermute(folded[k + 1], 'gy', pairs)  9.26 us
    ppermute x2, starting transfers between devices, body(): parts.append(lax.ppermute(folded[k + 1], 'gz', pairs))  7.43 us
    ppermute x4, waiting for transfers between devices, body(): lax.ppermute(block, axis, pairs)  6.73 us
    ppermute x2, waiting for transfers between devices, body(): parts.append(lax.ppermute(folded[k + 1], 'gz', pairs))  6.01 us
    unnamed x16, local copies, waits for them, and re-layouts  5.03 us
    pallas_call x1, Pallas kernels, body(): pl.pallas_call(functools.partial(main_kernel, count, even_slots), out_sha...  4.06 us
  transfers between devices with their start and end apart: 10, of which 6 were waited for; matrix products, arithmetic and copies ran while one was open for 3% of the time, Pallas kernels for 0%

profile of v1, /device:TPU:0, one launch (start us, length us, event | category | flops | bytes accessed | tf_op | source)
XLA Modules:
  0.0 77.6 jit_solution(14321857392433776984)
XLA Ops:
  0.6 1.3 %copy.12 = f32[1,1,1,2,3,128]{5,4,3,2,1,0:T(4,128)} copy(f32[1,1,1,2,3,128]{5,3,4,2,1,0:T(2,128)} %param.7) | data formatting | bytes 6144 | tf_op args[0]
  1.9 1.5 %pack.1 = bf16[2,144,128]{2,1,0:T(8,128)(2,1)} custom-call(s32[2]{0:T(128)} %bitcast.11, bf16[2,128,128]{2,1,0:T(8,128)(2,1)} %bitcast.8, f32[2,3,128]{2,1,0:T(4,128)} %bitcast.9), custom_call_target="tpu_custom_call" | custom-call | tf_op jit(solution)/shard_map/pack/pallas_call | solution.py:316
  3.4 0.7 collective-permute-start.1
  4.1 5.8 %collective-permute-start = (bf16[2,144,128]{2,1,0:T(8,128)(2,1)}, bf16[2,144,128]{2,1,0:T(8,128)(2,1)S(1)}, u32[]{:S(2)}, u32[]{:S(2)}) collective-permute-start(bf16[2,144,128]{2,1,0:T(8,128)(2,1)} %pack.1), channel_id=1, source_target_pairs={{0,1},{2,3},{1,0},{3,2},{4,5},{6,7},{5,4},{7,6},{8,9},{10,11},{9,8... | collective-permute-start | bytes 221192 | tf_op jit(solution)/shard_map/ppermute | solution.py:327
  9.9 0.9 %constant_dynamic-update-slice_fusion.4 = bf16[18,144,128]{2,1,0:T(8,128)(2,1)S(1)} fusion(bf16[2,144,128]{2,1,0:T(8,128)(2,1)} %pack.1), kind=kLoop, calls=%fused_computation.7 | loop fusion | bytes 147456
  10.8 2.8 %collective-permute-done = bf16[2,144,128]{2,1,0:T(8,128)(2,1)S(1)} collective-permute-done((bf16[2,144,128]{2,1,0:T(8,128)(2,1)}, bf16[2,144,128]{2,1,0:T(8,128)(2,1)S(1)}, u32[]{:S(2)}, u32[]{:S(2)}) %collective-permute-start) | collective-permute-done | bytes 73760 | tf_op jit(solution)/shard_map/ppermute | solution.py:327
  13.5 0.9 %pad_maximum_fusion = bf16[6,144,128]{2,1,0:T(8,128)(2,1)S(1)} fusion(bf16[2,144,128]{2,1,0:T(8,128)(2,1)S(1)} %collective-permute-done.1, bf16[2,144,128]{2,1,0:T(8,128)(2,1)S(1)} %collective-permute-done, bf16[2,144,128]{2,1,0:T(8,128)(2,1)} %pack.1), kind=kLoop, calls=%fused_computation.2 | loop fusion | flops 221184 | bytes 442368 | tf_op jit(solution)/shard_map/concatenate | solution.py:328
  14.5 0.7 collective-permute-start.3
  15.1 4.5 %collective-permute-start.2 = (bf16[6,144,128]{2,1,0:T(8,128)(2,1)S(1)}, bf16[6,144,128]{2,1,0:T(8,128)(2,1)S(1)}, u32[]{:S(2)}, u32[]{:S(2)}) collective-permute-start(bf16[6,144,128]{2,1,0:T(8,128)(2,1)S(1)} %pad_maximum_fusion), channel_id=1, source_target_pairs={{0,4},{8,12},{4,0},{12,8},{1,5},{9,13},{5,1},{13,9},{2,6},{10,14},... | collective-permute-start | bytes 663560 | tf_op jit(solution)/shard_map/ppermute | solution.py:327
  19.6 4.0 %collective-permute-done.2 = bf16[6,144,128]{2,1,0:T(8,128)(2,1)S(1)} collective-permute-done((bf16[6,144,128]{2,1,0:T(8,128)(2,1)S(1)}, bf16[6,144,128]{2,1,0:T(8,128)(2,1)S(1)}, u32[]{:S(2)}, u32[]{:S(2)}) %collective-permute-start.2) | collective-permute-done | bytes 221216 | tf_op jit(solution)/shard_map/ppermute | solution.py:327
  23.8 0.1 ne.71
  23.9 0.6 fusion.1
  24.5 0.1 rem.76
  24.6 0.1 div.19
  24.7 0.5 fusion.2.index_ref
  25.2 0.6 collective-permute-done.4.refs_1_
  25.9 0.8 %copy-done.1 = bf16[18,144,128]{2,1,0:T(8,128)(2,1)} copy-done((bf16[18,144,128]{2,1,0:T(8,128)(2,1)}, bf16[18,144,128]{2,1,0:T(8,128)(2,1)S(1)}, u32[]{:S(2)}) %copy-start.1) | copy-done | bytes 663576
  26.7 4.1 %pairs.1 = (f32[18,136,128]{2,1,0:T(8,128)}, f32[18,136,128]{2,1,0:T(8,128)}) custom-call(s32[2]{0:T(128)} %bitcast.12, s32[16]{0:T(128)} %fusion.2.index_ref, s32[2]{0:T(128)} %get-tuple-element.17.live_ref, f32[4]{0:T(128)} %rates_ref.1, f32[2,3,128]{2,1,0:T(4,128)} %bitcast.10, bf16[1024,128]{1,0:T(8,128)(2,1)} %mixing_ref.1, f32[1,128]{1,0:T(1,128)} %bitcast.15, ...), custom_call_target="tpu_custom_call" | custom-call | tf_op jit(solution)/shard_map/pairs/pallas_call | solution.py:350
  30.8 0.2 collective-permute-start.5
  31.0 3.0 %collective-permute-done.5 = f32[18,136,128]{2,1,0:T(8,128)S(1)} collective-permute-done((f32[18,136,128]{2,1,0:T(8,128)}, f32[18,136,128]{2,1,0:T(8,128)S(1)}, u32[]{:S(2)}, u32[]{:S(2)}) %collective-permute-start.5) | collective-permute-done | bytes 1253408 | tf_op jit(solution)/shard_map/ppermute | solution.py:386
  34.0 1.5 %add.69 = f32[18,136,128]{2,1,0:T(8,128)S(1)} add(f32[18,136,128]{2,1,0:T(8,128)} %get-tuple-element.6, f32[18,136,128]{2,1,0:T(8,128)S(1)} %collective-permute-done.5) | non-fusion elementwise | flops 313344 | bytes 3760128 | tf_op jit(solution)/shard_map/add | solution.py:386
  35.5 14.2 %collective-permute-start.6 = (f32[6,136,128]{2,1,0:T(8,128)S(1)}, f32[6,136,128]{2,1,0:T(8,128)S(1)}, u32[]{:S(2)}, u32[]{:S(2)}) collective-permute-start(f32[6,136,128]{2,1,0:T(8,128)S(1)} %get-tuple-element.12), channel_id=1, source_target_pairs={{0,4},{8,12},{4,0},{12,8},{1,5},{9,13},{5,1},{13,9},{2,6},{10,14},... | collective-permute-start | bytes 1253384 | tf_op jit(solution)/shard_map/ppermute | solution.py:391
  49.7 0.7 collective-permute-start.7
  50.4 9.3 %collective-permute-done.6 = f32[6,136,128]{2,1,0:T(8,128)S(1)} collective-permute-done((f32[6,136,128]{2,1,0:T(8,128)S(1)}, f32[6,136,128]{2,1,0:T(8,128)S(1)}, u32[]{:S(2)}, u32[]{:S(2)}) %collective-permute-start.6) | collective-permute-done | bytes 417824 | tf_op jit(solution)/shard_map/ppermute | solution.py:391
  59.7 0.1 fusion
  59.8 0.7 fusion.6
  60.5 0.7 collective-permute-start.9
  61.1 6.8 %collective-permute-start.8 = (f32[2,136,128]{2,1,0:T(8,128)S(1)}, f32[2,136,128]{2,1,0:T(8,128)S(1)}, u32[]{:S(2)}, u32[]{:S(2)}) collective-permute-start(f32[2,136,128]{2,1,0:T(8,128)S(1)} %get-tuple-element.15), channel_id=1, source_target_pairs={{0,1},{2,3},{1,0},{3,2},{4,5},{6,7},{5,4},{7,6},{8,9},{10,11},{9,8... | collective-permute-start | bytes 417800 | tf_op jit(solution)/shard_map/ppermute | solution.py:396
  67.9 6.0 %collective-permute-done.8.refs_1_ = f32[2,136,128]{2,1,0:T(8,128)S(1)} collective-permute-done((f32[2,136,128]{2,1,0:T(8,128)S(1)}, f32[2,136,128]{2,1,0:T(8,128)S(1)}, u32[]{:S(2)}, u32[]{:S(2)}) %collective-permute-start.8) | collective-permute-done | bytes 139296 | tf_op jit(solution)/shard_map/ppermute | solution.py:396
  73.9 0.6 copy-done.3
  74.6 1.8 %finish.1 = (f32[2,3,128]{2,1,0:T(4,128)}, f32[2,128,128]{2,1,0:T(8,128)}) custom-call(s32[2]{0:T(128)} %bitcast.13, f32[2,136,128]{2,1,0:T(8,128)} %get-tuple-element.16.refs_0_, f32[2,136,128]{2,1,0:T(8,128)} %copy-done.3, f32[2,136,128]{2,1,0:T(8,128)} %copy-done.2), custom_call_target="tpu_custom_call" | custom-call | tf_op jit(solution)/shard_map/finish/pallas_call | solution.py:398
  76.4 1.3 %copy.10 = f32[1,1,1,2,3,128]{5,3,4,2,1,0:T(2,128)} copy(f32[1,1,1,2,3,128]{5,4,3,2,1,0:T(4,128)} %bitcast.14) | data formatting | bytes 6144
  (19 shorter events, 0.3 us)
Async XLA Ops:
  0.6 23.1 %copy-start.4 = (s32[1,1,1,2,8]{4,3,2,1,0:T(2,128)S(1)}, s32[1,1,1,2,8]{4,3,2,1,0:T(2,128)}, u32[]{:S(2)}) copy-start(s32[1,1,1,2,8]{4,3,2,1,0:T(2,128)} %param.10) | copy-start | bytes 196
  3.4 7.4 %collective-permute-start.1 = (bf16[2,144,128]{2,1,0:T(8,128)(2,1)}, bf16[2,144,128]{2,1,0:T(8,128)(2,1)S(1)}, u32[]{:S(2)}, u32[]{:S(2)}) collective-permute-start(bf16[2,144,128]{2,1,0:T(8,128)(2,1)} %pack.1), channel_id=1, source_target_pairs={{1,2},{2,1},{5,6},{6,5},{9,10},{10,9},{13,14},{14,13},{17,18},{18,... | collective-permute-start | bytes 221192 | tf_op jit(solution)/shard_map/ppermute | solution.py:327
  4.1 9.5 %collective-permute-start = (bf16[2,144,128]{2,1,0:T(8,128)(2,1)}, bf16[2,144,128]{2,1,0:T(8,128)(2,1)S(1)}, u32[]{:S(2)}, u32[]{:S(2)}) collective-permute-start(bf16[2,144,128]{2,1,0:T(8,128)(2,1)} %pack.1), channel_id=1, source_target_pairs={{0,1},{2,3},{1,0},{3,2},{4,5},{6,7},{5,4},{7,6},{8,9},{10,11},{9,8... | collective-permute-start | bytes 221192 | tf_op jit(solution)/shard_map/ppermute | solution.py:327
  14.5 9.2 %collective-permute-start.3 = (bf16[6,144,128]{2,1,0:T(8,128)(2,1)S(1)}, bf16[6,144,128]{2,1,0:T(8,128)(2,1)S(1)}, u32[]{:S(2)}, u32[]{:S(2)}) collective-permute-start(bf16[6,144,128]{2,1,0:T(8,128)(2,1)S(1)} %pad_maximum_fusion), channel_id=1, source_target_pairs={{4,8},{8,4},{5,9},{9,5},{6,10},{10,6},{7,11},{11,7},{20,24},{24,20... | collective-permute-start | bytes 663560 | tf_op jit(solution)/shard_map/ppermute | solution.py:327
  15.1 8.4 %collective-permute-start.2 = (bf16[6,144,128]{2,1,0:T(8,128)(2,1)S(1)}, bf16[6,144,128]{2,1,0:T(8,128)(2,1)S(1)}, u32[]{:S(2)}, u32[]{:S(2)}) collective-permute-start(bf16[6,144,128]{2,1,0:T(8,128)(2,1)S(1)} %pad_maximum_fusion), channel_id=1, source_target_pairs={{0,4},{8,12},{4,0},{12,8},{1,5},{9,13},{5,1},{13,9},{2,6},{10,14},... | collective-permute-start | bytes 663560 | tf_op jit(solution)/shard_map/ppermute | solution.py:327
  23.7 2.2 %copy-start = (bf16[18,144,128]{2,1,0:T(8,128)(2,1)}, bf16[18,144,128]{2,1,0:T(8,128)(2,1)S(1)}, u32[]{:S(2)}) copy-start(bf16[18,144,128]{2,1,0:T(8,128)(2,1)S(1)} %constant_dynamic-update-slice_fusion.refs_0_) | copy-start | bytes 1990660
  23.7 2.2 %collective-permute-start.4 = (bf16[18,144,128]{2,1,0:T(8,128)(2,1)S(1)}, bf16[18,144,128]{2,1,0:T(8,128)(2,1)S(1)}, u32[]{:S(2)}, u32[]{:S(2)}) collective-permute-start(bf16[18,144,128]{2,1,0:T(8,128)(2,1)S(1)} %constant_dynamic-update-slice_fusion.refs_0_), channel_id=1, source_target_pairs={{0,16},{16,0},{1,17},{17,1},{2,18},{18,2},{3,19},{19,3},{4,20},{20... | collective-permute-start | bytes 1990664 | tf_op jit(solution)/shard_map/ppermute | solution.py:329
  25.9 0.8 %copy-start.1 = (bf16[18,144,128]{2,1,0:T(8,128)(2,1)}, bf16[18,144,128]{2,1,0:T(8,128)(2,1)S(1)}, u32[]{:S(2)}) copy-start(bf16[18,144,128]{2,1,0:T(8,128)(2,1)S(1)} %collective-permute-done.4.refs_1_) | copy-start | bytes 1990660
  30.8 3.2 %collective-permute-start.5 = (f32[18,136,128]{2,1,0:T(8,128)}, f32[18,136,128]{2,1,0:T(8,128)S(1)}, u32[]{:S(2)}, u32[]{:S(2)}) collective-permute-start(f32[18,136,128]{2,1,0:T(8,128)} %get-tuple-element.7), channel_id=1, source_target_pairs={{0,16},{16,0},{1,17},{17,1},{2,18},{18,2},{3,19},{19,3},{4,20},{20... | collective-permute-start | bytes 3760136 | tf_op jit(solution)/shard_map/ppermute | solution.py:386
  35.5 24.1 %collective-permute-start.6 = (f32[6,136,128]{2,1,0:T(8,128)S(1)}, f32[6,136,128]{2,1,0:T(8,128)S(1)}, u32[]{:S(2)}, u32[]{:S(2)}) collective-permute-start(f32[6,136,128]{2,1,0:T(8,128)S(1)} %get-tuple-element.12), channel_id=1, source_target_pairs={{0,4},{8,12},{4,0},{12,8},{1,5},{9,13},{5,1},{13,9},{2,6},{10,14},... | collective-permute-start | bytes 1253384 | tf_op jit(solution)/shard_map/ppermute | solution.py:391
  49.7 9.9 %collective-permute-start.7 = (f32[6,136,128]{2,1,0:T(8,128)S(1)}, f32[6,136,128]{2,1,0:T(8,128)S(1)}, u32[]{:S(2)}, u32[]{:S(2)}) collective-permute-start(f32[6,136,128]{2,1,0:T(8,128)S(1)} %get-tuple-element.13), channel_id=1, source_target_pairs={{4,8},{8,4},{5,9},{9,5},{6,10},{10,6},{7,11},{11,7},{20,24},{24,20... | collective-permute-start | bytes 1253384 | tf_op jit(solution)/shard_map/ppermute | solution.py:391
  60.5 7.4 %collective-permute-start.9 = (f32[2,136,128]{2,1,0:T(8,128)S(1)}, f32[2,136,128]{2,1,0:T(8,128)S(1)}, u32[]{:S(2)}, u32[]{:S(2)}) collective-permute-start(f32[2,136,128]{2,1,0:T(8,128)S(1)} %get-tuple-element.14), channel_id=1, source_target_pairs={{1,2},{2,1},{5,6},{6,5},{9,10},{10,9},{13,14},{14,13},{17,18},{18,... | collective-permute-start | bytes 417800 | tf_op jit(solution)/shard_map/ppermute | solution.py:396
  61.1 12.8 %collective-permute-start.8 = (f32[2,136,128]{2,1,0:T(8,128)S(1)}, f32[2,136,128]{2,1,0:T(8,128)S(1)}, u32[]{:S(2)}, u32[]{:S(2)}) collective-permute-start(f32[2,136,128]{2,1,0:T(8,128)S(1)} %get-tuple-element.15), channel_id=1, source_target_pairs={{0,1},{2,3},{1,0},{3,2},{4,5},{6,7},{5,4},{7,6},{8,9},{10,11},{9,8... | collective-permute-start | bytes 417800 | tf_op jit(solution)/shard_map/ppermute | solution.py:396
  67.9 6.0 %copy-start.2 = (f32[2,136,128]{2,1,0:T(8,128)}, f32[2,136,128]{2,1,0:T(8,128)S(1)}, u32[]{:S(2)}) copy-start(f32[2,136,128]{2,1,0:T(8,128)S(1)} %collective-permute-done.9.refs_2_) | copy-start | bytes 417796
  73.9 0.7 copy-start.3
